TPU v7x, 32 devices: a whole 2x2x4 slice. The times are simulated.
32 devices in a mesh: prompt: 2 (over x), head: 16 (over z, y, core).
Axes of the slice: x: 2, y: 2, z: 4, core: 2. Of those that a mesh axis runs over, the one named last changes fastest.
Arguments:
- queries: bfloat16 [8192, 128], P(('prompt', 'head')), may hold values from -1.5 to 1.5
- out_grad: bfloat16 [8192, 128], P(('prompt', 'head')), may hold values from -6 to 6
- row_route: int32 [8192, 1], P(('prompt', 'head')), may hold values from 0 to 63; in each aligned block of 256 rows (0 to 255, 256 to 511, ...) at most 8 rows name the same one
- row_live: int32 [8192], P(('prompt', 'head')), may hold values 0 or 1
- states: bfloat16 [2, 4128, 8192], P('prompt', None, 'head'), may hold values from -0.14941406 to 0.14941406
Outputs:
- query_grad: bfloat16 [8192, 128], P(('prompt', 'head'))
- state_grad: float32 [2, 4128, 8192], P('prompt', None, 'head')
Inputs may be any that keep to these rules, and one draw needn't show every extreme that they name: `row_route`: among the 256 rows of one device no value appears more than 8 times, and some value appears exactly 8 times.
All inputs are finite; a program needn't handle non-finite values. No bound on the sum of `row_live` on one device may be relied on, other than what follows from the above.
Results may differ from a plain program's by a relative error of at most 0.0029.
Values may be sent and summed in bfloat16 or wider, within the bound.
No kernel may reach another device: no remote copies, remote signals or barrier semaphores. Data moves between devices by JAX's collectives and lax.ppermute only.
A program may use at most 128 MiB of HBM per device.

v0:
```python
import functools

import jax
import jax.numpy as jnp
import numpy as np
from jax import lax
from jax.experimental import pallas as pl
from jax.experimental.pallas import tpu as pltpu
from jax.sharding import PartitionSpec as P

KVH = 32


def score_grads(query_rows, grad_rows, sym_block, diag_block, mask_table):
    row_count, head_dim = query_rows.shape
    col_width = grad_rows.shape[1]
    block_rows = min(256, row_count)
    root_two = float(np.sqrt(2.0))
    query_blocks = query_rows.reshape(row_count // block_rows, block_rows, head_dim)
    grad_blocks = grad_rows.reshape(row_count // block_rows, block_rows, col_width)
    diag_float = diag_block.astype(jnp.float32)

    def block_step(total_grad, pair):
        query_block, grad_block = pair
        query_float = query_block.astype(jnp.float32)
        square = query_float[:, :, None] * query_float[:, None, :] * mask_table
        stored = square.reshape(block_rows, head_dim * head_dim).astype(jnp.bfloat16)
        total_grad = total_grad + lax.dot_general(
            stored, grad_block, (((0,), (0,)), ((), ())), preferred_element_type=jnp.float32
        )
        sweep = jnp.dot(query_block, sym_block, preferred_element_type=jnp.float32).reshape(
            block_rows, head_dim, col_width
        )
        sweep = (
            root_two * sweep
            - (2.0 * root_two - 2.0) * query_float[:, :, None] * diag_float[None, :, :]
        )
        grad_float = grad_block.astype(jnp.float32)
        query_part = jnp.einsum("baj,bj->ba", sweep, grad_float, precision=lax.Precision.HIGHEST)
        return (total_grad, query_part)

    start_grad = jnp.zeros((head_dim * head_dim, col_width), jnp.float32)
    total_grad, query_parts = lax.scan(block_step, start_grad, (query_blocks, grad_blocks))
    return (query_parts.reshape(row_count, head_dim), total_grad)


def general_device(queries, out_grad, row_route, row_live, states):
    prompt_count = lax.axis_size("prompt")
    head_count = lax.axis_size("head")
    rows_here, head_dim = queries.shape
    half_feat = states.shape[1]
    feat_count = 2 * half_feat
    column_count = states.shape[2] // 2
    kv_heads = KVH
    col_width = min(column_count, head_dim)
    copies = head_dim // col_width
    heads_held = column_count // col_width
    groups = prompt_count * kv_heads
    capacity = 2 * rows_here // groups
    first_index, second_index = np.triu_indices(head_dim)
    dense_place = (first_index * head_dim + second_index).astype(np.int32)
    triangle_of = np.full(head_dim * head_dim, feat_count, np.int32)
    triangle_of[dense_place] = np.arange(feat_count, dtype=np.int32)
    diagonal_of = triangle_of[np.arange(head_dim) * head_dim + np.arange(head_dim)]
    mask_np = np.zeros((head_dim, head_dim), np.float32)
    mask_np[first_index, second_index] = np.where(first_index == second_index, 1.0, np.sqrt(2.0))
    mask_table = jnp.asarray(mask_np)
    route_ids = row_route[:, 0]
    one_hot = (route_ids[:, None] == jnp.arange(groups, dtype=jnp.int32)[None, :]).astype(jnp.int32)
    slot_rank = jnp.sum(jnp.cumsum(one_hot, axis=0) * one_hot, axis=1) - 1
    slot_place = route_ids * capacity + slot_rank
    live_mask = row_live.astype(jnp.float32)[:, None]
    query_live = (queries.astype(jnp.float32) * live_mask).astype(jnp.bfloat16)
    grad_live = (out_grad.astype(jnp.float32) * live_mask).astype(jnp.bfloat16)
    query_bucket = (
        jnp.zeros((groups * capacity, head_dim), jnp.bfloat16).at[slot_place].set(query_live)
    )
    grad_bucket = (
        jnp.zeros((groups * capacity, head_dim), jnp.bfloat16).at[slot_place].set(grad_live)
    )
    query_send = jnp.broadcast_to(
        query_bucket.reshape(prompt_count, kv_heads, 1, capacity, head_dim),
        (prompt_count, kv_heads, copies, capacity, head_dim),
    )
    query_send = query_send.reshape(prompt_count, head_count, heads_held * capacity, head_dim)
    grad_send = grad_bucket.reshape(prompt_count, kv_heads, capacity, copies, col_width).transpose(
        0, 1, 3, 2, 4
    )
    grad_send = grad_send.reshape(prompt_count, head_count, heads_held * capacity, col_width)
    sectioned_query, sectioned_grad = (
        lax.all_to_all(query_send, "head", split_axis=1, concat_axis=1, tiled=True),
        lax.all_to_all(grad_send, "head", split_axis=1, concat_axis=1, tiled=True),
    )
    query_recv, grad_recv = (
        lax.all_to_all(sectioned_query, "prompt", split_axis=0, concat_axis=0, tiled=True),
        lax.all_to_all(sectioned_grad, "prompt", split_axis=0, concat_axis=0, tiled=True),
    )
    query_items = query_recv.reshape(prompt_count * head_count, heads_held, capacity, head_dim)
    grad_items = grad_recv.reshape(prompt_count * head_count, heads_held, capacity, col_width)
    local_state = (
        states[0]
        .reshape(half_feat, column_count, 2)
        .transpose(0, 2, 1)
        .reshape(feat_count, column_count)
    )
    padded_state = jnp.concatenate(
        [local_state, jnp.zeros((1, column_count), local_state.dtype)], axis=0
    )
    upper_state = padded_state[triangle_of].reshape(head_dim, head_dim, column_count)
    sym_state = upper_state + jnp.swapaxes(upper_state, 0, 1)
    diag_state = local_state[diagonal_of]
    query_shares = []
    state_shares = []
    for index in range(heads_held):
        query_rows = query_items[:, index].reshape(-1, head_dim)
        grad_rows = grad_items[:, index].reshape(-1, col_width)
        sym_block = sym_state[:, :, index * col_width : (index + 1) * col_width].reshape(
            head_dim, head_dim * col_width
        )
        diag_block = diag_state[:, index * col_width : (index + 1) * col_width]
        query_part, dense_grad = score_grads(
            query_rows, grad_rows, sym_block, diag_block, mask_table
        )
        query_shares.append(query_part.reshape(prompt_count * head_count, capacity, head_dim))
        state_shares.append(dense_grad[dense_place])
    query_partial = jnp.stack(query_shares, axis=1).reshape(
        prompt_count, head_count, heads_held * capacity, head_dim
    )
    state_full = jnp.concatenate(state_shares, axis=1)
    state_grad = (
        state_full.reshape(half_feat, 2, column_count)
        .transpose(0, 2, 1)
        .reshape(1, half_feat, 2 * column_count)
    )
    halfway = lax.all_to_all(query_partial, "head", split_axis=1, concat_axis=1, tiled=True)
    returned = lax.all_to_all(halfway, "prompt", split_axis=0, concat_axis=0, tiled=True)
    query_total = jnp.sum(
        returned.reshape(prompt_count, kv_heads, copies, capacity, head_dim), axis=2
    )
    query_grad = query_total.reshape(groups * capacity, head_dim)[slot_place].astype(jnp.bfloat16)
    return (query_grad, state_grad)


LANES = 128
SUB = 8


def pair_runs(head_dim):
    runs = []
    for a in range(head_dim):
        offset = a * head_dim - a * (a - 1) // 2
        for parity in range(2):
            b = a + (parity - offset) % 2
            if b < head_dim:
                first = (offset + b - a - parity) // 2
                runs.append((a, parity, b & 1, b >> 1, first, b == a))
    return runs


def split_place(index, head_dim):
    return (index & 1) * (head_dim // 2) + (index >> 1)


def eye_of(size, dtype=jnp.float32):
    return (
        lax.broadcasted_iota(jnp.int32, (size, size), 0)
        == lax.broadcasted_iota(jnp.int32, (size, size), 1)
    )


def parity_split(size):
    row = lax.broadcasted_iota(jnp.int32, (size, size), 0)
    col = lax.broadcasted_iota(jnp.int32, (size, size), 1)
    half = size // 2
    wanted = jnp.where(row < half, 2 * row, 2 * (row - half) + 1)
    return (col == wanted).astype(jnp.bfloat16)


def slot_row(route, rows, capacity):
    eye = eye_of(rows)
    wide = jnp.broadcast_to(route, (rows, rows))
    column = jnp.sum(jnp.where(eye, wide, 0), axis=1, keepdims=True)
    first = lax.broadcasted_iota(jnp.int32, (rows, rows), 0)
    second = lax.broadcasted_iota(jnp.int32, (rows, rows), 1)
    earlier = (column == wide) & (first < second)
    rank = jnp.sum(earlier.astype(jnp.int32), axis=0, keepdims=True)
    return route * capacity + rank


def pack_kernel(capacity, route_ref, live_ref, query_ref, grad_ref, send_ref):
    rows, head_dim = query_ref.shape
    slots = send_ref.shape[0]
    place = slot_row(route_ref[...], rows, capacity)
    place = jnp.where(live_ref[...] != 0, place, -1)
    pick = lax.broadcasted_iota(jnp.int32, (slots, rows), 0) == place
    pick = pick.astype(jnp.float32).astype(jnp.bfloat16)
    send_ref[:, :head_dim] = jnp.dot(
        pick, query_ref[...], preferred_element_type=jnp.float32
    ).astype(jnp.bfloat16)
    send_ref[:, head_dim:] = jnp.dot(
        pick, grad_ref[...], preferred_element_type=jnp.float32
    ).astype(jnp.bfloat16)


def unpack_kernel(capacity, route_ref, back_ref, out_ref):
    rows, head_dim = out_ref.shape
    slots = back_ref.shape[0]
    place = slot_row(route_ref[...], rows, capacity)
    eye = eye_of(rows)
    column = jnp.sum(
        jnp.where(eye, jnp.broadcast_to(place, (rows, rows)), 0), axis=1, keepdims=True
    )
    pick = lax.broadcasted_iota(jnp.int32, (rows, slots), 1) == column
    pick = pick.astype(jnp.float32).astype(jnp.bfloat16)
    out_ref[...] = jnp.dot(
        pick, back_ref[...], preferred_element_type=jnp.float32
    ).astype(jnp.bfloat16)


def head_rows(recv_ref, head, heads_held, capacity):
    slots, width = recv_ref.shape
    whole = recv_ref[...].astype(jnp.float32)
    split = whole.reshape(slots // (heads_held * capacity), heads_held, capacity, width)
    return split[:, head].reshape(slots // heads_held, width).astype(jnp.bfloat16)


def stuff_transposed(grad, parity):
    width = grad.shape[1]
    row = lax.broadcasted_iota(jnp.int32, (2 * width, width), 0)
    col = lax.broadcasted_iota(jnp.int32, (2 * width, width), 1)
    place = (row == 2 * col + parity).astype(jnp.bfloat16)
    return lax.dot_general(
        place, grad, (((1,), (1,)), ((), ())), preferred_element_type=jnp.float32
    ).astype(jnp.bfloat16)


def stuff(grad, parity):
    width = grad.shape[1]
    row = lax.broadcasted_iota(jnp.int32, (width, 2 * width), 0)
    col = lax.broadcasted_iota(jnp.int32, (width, 2 * width), 1)
    place = (col == 2 * row + parity).astype(jnp.bfloat16)
    return jnp.dot(grad, place, preferred_element_type=jnp.float32).astype(jnp.bfloat16)


def split_query(query):
    return lax.dot_general(
        parity_split(query.shape[1]),
        query,
        (((1,), (1,)), ((), ())),
        preferred_element_type=jnp.float32,
    )


def run_weight(start, diagonal, on_diagonal, off_diagonal):
    row = lax.broadcasted_iota(jnp.int32, (SUB, LANES), 0)
    value = jnp.where(row >= start, jnp.float32(off_diagonal), jnp.float32(0.0))
    if diagonal:
        value = jnp.where(row == start, jnp.float32(on_diagonal), value)
    return value


def query_kernel(
    heads_held, capacity, chunk, states_ref, recv_ref, out_ref,
    state_buf, xt_ref, feat_ref, acc_ref, dqt_ref, sem,
):
    half_feat, lanes = states_ref.shape
    slots, width = recv_ref.shape
    head_dim = width // 2
    half = head_dim // 2
    wide = lanes // heads_held
    rows = slots // heads_held
    cols = rows // LANES
    steps = half_feat // chunk
    copies = [
        pltpu.make_async_copy(
            states_ref.at[pl.ds(i * chunk, chunk)], state_buf.at[pl.ds(i * chunk, chunk)], sem.at[i]
        )
        for i in range(steps)
    ]
    for copy in copies:
        copy.start()
    stuffed = []
    for head in range(heads_held):
        block = head_rows(recv_ref, head, heads_held, capacity)
        grad = block[:, head_dim:]
        stuffed.append([stuff_transposed(grad, 0), stuff_transposed(grad, 1)])
        turned = split_query(block[:, :head_dim])
        for col in range(cols):
            xt_ref[head * cols + col] = turned[:, col * LANES : (col + 1) * LANES]
    for i in range(steps):
        copies[i].wait()
        for head in range(heads_held):
            part = state_buf[i * chunk : (i + 1) * chunk, head * wide : (head + 1) * wide]
            for parity in range(2):
                feat = jnp.dot(part, stuffed[head][parity], preferred_element_type=jnp.float32)
                for col in range(cols):
                    feat_ref[head * cols + col, parity, i * chunk : (i + 1) * chunk, :] = feat[
                        :, col * LANES : (col + 1) * LANES
                    ]
    runs = pair_runs(head_dim)
    regs = half // SUB
    inv_root = float(np.sqrt(0.5))

    def column(t, carry):
        values = [[xt_ref[t, p * half + m * SUB : p * half + (m + 1) * SUB, :] for m in range(regs)] for p in range(2)]
        totals = [[jnp.zeros((SUB, LANES), jnp.float32) for _ in range(regs)] for _ in range(2)]
        for a in range(head_dim):
            at = split_place(a, head_dim)
            own = jnp.broadcast_to(xt_ref[t, at : at + 1, :], (SUB, LANES))
            acc = None
            for owner, parity, side, start, first, diagonal in runs:
                if owner != a:
                    continue
                for m in range(start // SUB, regs):
                    place = first - start + m * SUB
                    feat = feat_ref[t, parity, place : place + SUB, :]
                    if m == start // SUB and (start % SUB or diagonal):
                        feat = feat * run_weight(start % SUB, diagonal, inv_root, 1.0)
                    term = feat * values[side][m]
                    acc = term if acc is None else acc + term
                    totals[side][m] = totals[side][m] + feat * own
            acc_ref[at * SUB : (at + 1) * SUB, :] = acc
        root = float(np.sqrt(2.0))
        for p in range(2):
            for m in range(regs):
                total = totals[p][m]
                base = (p * half + m * SUB) * SUB
                for k in range(SUB):
                    total = total + acc_ref[pl.ds(base + k, SUB, stride=SUB), :]
                dqt_ref[t, p * half + m * SUB : p * half + (m + 1) * SUB, :] = total * root
        return carry

    lax.fori_loop(0, heads_held * cols, column, 0)
    back = parity_split(head_dim)
    pieces = []
    for head in range(heads_held):
        turned = jnp.concatenate([dqt_ref[head * cols + col] for col in range(cols)], axis=1)
        part = lax.dot_general(
            turned.astype(jnp.bfloat16), back, (((0,), (0,)), ((), ())), preferred_element_type=jnp.float32
        )
        pieces.append(part.reshape(rows // capacity, 1, capacity, head_dim))
    out_ref[...] = jnp.concatenate(pieces, axis=1).reshape(slots, head_dim).astype(out_ref.dtype)


def state_kernel(
    heads_held, capacity, chunk, recv_ref, out_ref, xt_ref, feat_ref, stuffed_ref, out_buf, sem
):
    half_feat, lanes = out_ref.shape
    slots, width = recv_ref.shape
    head_dim = width // 2
    half = head_dim // 2
    wide = lanes // heads_held
    rows = slots // heads_held
    cols = rows // LANES
    steps = half_feat // chunk
    runs = pair_runs(head_dim)
    regs = half // SUB
    root = float(np.sqrt(2.0))
    for head in range(heads_held):
        block = head_rows(recv_ref, head, heads_held, capacity)
        grad = block[:, head_dim:]
        for parity in range(2):
            stuffed_ref[head, parity * rows : (parity + 1) * rows, :] = stuff(grad, parity)
        turned = split_query(block[:, :head_dim])
        for col in range(cols):
            xt_ref[head * cols + col] = turned[:, col * LANES : (col + 1) * LANES]

    def store_of(head, i):
        return pltpu.make_async_copy(
            out_buf.at[head, pl.ds(i * chunk, chunk)],
            out_ref.at[pl.ds(i * chunk, chunk), pl.ds(head * wide, wide)],
            sem.at[head, i],
        )

    for head in range(heads_held):

        def column(col, carry):
            t = head * cols + col
            values = [[xt_ref[t, p * half + m * SUB : p * half + (m + 1) * SUB, :] for m in range(regs)] for p in range(2)]
            for a, parity, side, start, first, diagonal in reversed(runs):
                at = split_place(a, head_dim)
                own = jnp.broadcast_to(xt_ref[t, at : at + 1, :], (SUB, LANES))
                for m in range(start // SUB, regs):
                    place = first - start + m * SUB
                    value = values[side][m] * own
                    if diagonal and m == start // SUB:
                        value = value * run_weight(start % SUB, True, 1.0, root)
                    else:
                        value = value * root
                    feat_ref[col, parity, place : place + SUB, :] = value
            return carry

        lax.fori_loop(0, cols, column, 0)

        def product(i, carry):
            at = pl.multiple_of(i * chunk, chunk)
            parts = [
                feat_ref[col, parity, pl.ds(at, chunk), :].astype(jnp.bfloat16)
                for parity in range(2)
                for col in range(cols)
            ]
            out_buf[head, pl.ds(at, chunk), :] = jnp.dot(
                jnp.concatenate(parts, axis=1), stuffed_ref[head], preferred_element_type=jnp.float32
            )
            store_of(head, i).start()
            return carry

        lax.fori_loop(0, steps, product, 0)

    def drain(i, carry):
        for head in range(heads_held):
            store_of(head, i).wait()
        return carry

    lax.fori_loop(0, steps, drain, 0)


def fast_device(queries, out_grad, row_route, row_live, states):
    axes = ("prompt", "head")
    prompt_count = lax.axis_size("prompt")
    rows_here, head_dim = queries.shape
    half_feat = states.shape[1]
    column_count = states.shape[2] // 2
    heads_held = column_count // head_dim
    groups = prompt_count * KVH
    capacity = 2 * rows_here // groups
    slots = groups * capacity
    chunk = half_feat // 6
    cols = slots // heads_held // LANES
    vmem = pl.BlockSpec(memory_space=pltpu.VMEM)
    hbm = pl.BlockSpec(memory_space=pl.ANY)
    params = pltpu.CompilerParams(vmem_limit_bytes=60 * 1024 * 1024)
    route = row_route.reshape(1, rows_here)
    live = row_live.reshape(1, rows_here)
    send = pl.pallas_call(
        functools.partial(pack_kernel, capacity),
        out_shape=jax.ShapeDtypeStruct((slots, 2 * head_dim), jnp.bfloat16),
        in_specs=[vmem] * 4,
        out_specs=vmem,
        name="pack_rows",
    )(route, live, queries, out_grad)
    recv = lax.all_to_all(send, axes, split_axis=0, concat_axis=0, tiled=True)
    answer = pl.pallas_call(
        functools.partial(query_kernel, heads_held, capacity, chunk),
        out_shape=jax.ShapeDtypeStruct((slots, head_dim), jnp.bfloat16),
        in_specs=[hbm, vmem],
        out_specs=vmem,
        scratch_shapes=[
            pltpu.VMEM((half_feat, 2 * column_count), jnp.bfloat16),
            pltpu.VMEM((heads_held * cols, head_dim, LANES), jnp.float32),
            pltpu.VMEM((heads_held * cols, 2, half_feat, LANES), jnp.float32),
            pltpu.VMEM((head_dim * SUB, LANES), jnp.float32),
            pltpu.VMEM((heads_held * cols, head_dim, LANES), jnp.float32),
            pltpu.SemaphoreType.DMA((half_feat // chunk,)),
        ],
        compiler_params=params,
        name="query_side",
    )(states[0], recv)
    back = lax.all_to_all(answer, axes, split_axis=0, concat_axis=0, tiled=True)
    state_grad = pl.pallas_call(
        functools.partial(state_kernel, heads_held, capacity, chunk),
        out_shape=jax.ShapeDtypeStruct((half_feat, 2 * column_count), jnp.float32),
        in_specs=[vmem],
        out_specs=hbm,
        scratch_shapes=[
            pltpu.VMEM((heads_held * cols, head_dim, LANES), jnp.float32),
            pltpu.VMEM((cols, 2, half_feat, LANES), jnp.float32),
            pltpu.VMEM((heads_held, 2 * slots // heads_held, 2 * head_dim), jnp.bfloat16),
            pltpu.VMEM((heads_held, half_feat, 2 * head_dim), jnp.float32),
            pltpu.SemaphoreType.DMA((heads_held, half_feat // chunk)),
        ],
        compiler_params=params,
        name="state_side",
    )(recv)
    query_grad = pl.pallas_call(
        functools.partial(unpack_kernel, capacity),
        out_shape=jax.ShapeDtypeStruct((rows_here, head_dim), jnp.bfloat16),
        in_specs=[vmem] * 2,
        out_specs=vmem,
        name="unpack_rows",
    )(route, back)
    return (query_grad, state_grad[None])


def whole_heads(queries, states):
    rows_here, head_dim = queries.shape
    groups = lax.axis_size("prompt") * KVH
    capacity = 2 * rows_here // groups
    column_count = states.shape[2] // 2
    heads_held = column_count // head_dim
    return (
        head_dim == LANES
        and heads_held >= 1
        and column_count % head_dim == 0
        and capacity % SUB == 0
        and (groups * capacity // heads_held) % LANES == 0
        and states.shape[1] % 96 == 0
    )


def per_device(*arrays):
    if whole_heads(arrays[0], arrays[4]):
        return fast_device(*arrays)
    return general_device(*arrays)


def solution(mesh):
    return jax.shard_map(
        per_device,
        mesh=mesh,
        in_specs=(
            P(("prompt", "head"), None),
            P(("prompt", "head"), None),
            P(("prompt", "head"), None),
            P(("prompt", "head")),
            P("prompt", None, "head"),
        ),
        out_specs=(P(("prompt", "head"), None), P("prompt", None, "head")),
        check_vma=False,
    )
```

profile of v0, /device:TPU:0, one launch (start us, length us, event | category | flops | bytes accessed | tf_op | source)
XLA Modules:
  0.0 42.8 jit_solution(3584218888765892978)
XLA Ops:
  0.6 2.0 %pack_rows.1 = bf16[512,256]{1,0:T(8,128)(2,1)} custom-call(s32[1,256]{1,0:T(1,128)} %bitcast.15, s32[1,256]{1,0:T(1,128)} %bitcast.17, bf16[256,128]{1,0:T(8,128)(2,1)} %query_ref.1, bf16[256,128]{1,0:T(8,128)(2,1)} %grad_ref.1), custom_call_target="tpu_custom_call" | custom-call | tf_op jit(solution)/shard_map/pack_rows/pallas_call | solution.py:435
  2.7 17.7 %all_to_all.22 = bf16[32,16,256]{2,1,0:T(8,128)(2,1)} all-to-all(bf16[32,16,256]{2,1,0:T(8,128)(2,1)} %bitcast.12), channel_id=1, replica_groups=mesh['prompt'=2,'head'=16] {'prompt','head'}, dimensions={0} | all-to-all | bytes 524288 | tf_op jit(solution)/shard_map/all_to_all | solution.py:442
  20.4 9.0 %query_side.1 = bf16[512,128]{1,0:T(8,128)(2,1)} custom-call(bf16[4128,512]{1,0:T(8,128)(2,1)} %bitcast.9, bf16[512,256]{1,0:T(8,128)(2,1)} %bitcast.10), custom_call_target="tpu_custom_call" | custom-call | tf_op jit(solution)/shard_map/query_side/pallas_call | solution.py:443
  29.3 2.6 %all-to-all-start.1 = ((bf16[32,16,128]{2,1,0:T(8,128)(2,1)}), bf16[32,16,128]{2,1,0:T(8,128)(2,1)S(1)}, u32[]{:S(2)}, u32[]{:S(2)}) async-start(bf16[32,16,128]{2,1,0:T(8,128)(2,1)} %bitcast.13), calls=%async_computation.1 | async-start | bytes 262144 | tf_op jit(solution)/shard_map/all_to_all | solution.py:459
  31.9 7.8 %state_side.1 = f32[4128,512]{1,0:T(8,128)} custom-call(bf16[512,256]{1,0:T(8,128)(2,1)} %bitcast.11), custom_call_target="tpu_custom_call" | custom-call | tf_op jit(solution)/shard_map/state_side/pallas_call | solution.py:460
  39.8 0.4 all-to-all-done.1
  40.1 0.0 copy-start
  40.1 0.6 %copy-done = bf16[32,16,128]{2,1,0:T(8,128)(2,1)} copy-done((bf16[32,16,128]{2,1,0:T(8,128)(2,1)}, bf16[32,16,128]{2,1,0:T(8,128)(2,1)S(1)}, u32[]{:S(2)}) %copy-start) | copy-done | bytes 131096
  40.8 2.0 %unpack_rows.1 = bf16[256,128]{1,0:T(8,128)(2,1)} custom-call(s32[1,256]{1,0:T(1,128)} %bitcast.16, bf16[512,128]{1,0:T(8,128)(2,1)} %bitcast.14), custom_call_target="tpu_custom_call" | custom-call | tf_op jit(solution)/shard_map/unpack_rows/pallas_call | solution.py:475
Async XLA Ops:
  29.3 10.8 %all-to-all-start.1 = ((bf16[32,16,128]{2,1,0:T(8,128)(2,1)}), bf16[32,16,128]{2,1,0:T(8,128)(2,1)S(1)}, u32[]{:S(2)}, u32[]{:S(2)}) async-start(bf16[32,16,128]{2,1,0:T(8,128)(2,1)} %bitcast.13), calls=%async_computation.1 | async-start | bytes 262144 | tf_op jit(solution)/shard_map/all_to_all | solution.py:459
  40.1 0.6 %copy-start = (bf16[32,16,128]{2,1,0:T(8,128)(2,1)}, bf16[32,16,128]{2,1,0:T(8,128)(2,1)S(1)}, u32[]{:S(2)}) copy-start(bf16[32,16,128]{2,1,0:T(8,128)(2,1)S(1)} %all-to-all-done.1) | copy-start | bytes 393220
where the time goes:
time: 43.1 us; the launch traced here: 42.8 us
  Pallas kernels  20.9 us (48%)
  blocking collectives  17.7 us (41%)
  starting transfers between devices  2.58 us (6%)
  between operations  0.66 us (2%)
  local copies, waits for them, and re-layouts  0.65 us (2%)
    all_to_all x1, blocking collectives, fast_device(): recv = lax.all_to_all(send, axes, split_axis=0, concat_axis=0, tiled=True)  17.7 us
    pallas_call x1, Pallas kernels, fast_device(): pl.pallas_call(functools.partial(query_kernel, heads_held, capacity, chun...  8.97 us
    pallas_call x1, Pallas kernels, fast_device(): pl.pallas_call(functools.partial(state_kernel, heads_held, capacity, chun...  7.84 us
    all_to_all x1, starting transfers between devices, fast_device(): back = lax.all_to_all(answer, axes, split_axis=0, concat_axis=0, tiled=True)  2.58 us
    pallas_call x1, Pallas kernels, fast_device(): pl.pallas_call(functools.partial(pack_kernel, capacity), out_shape=jax.Sh...  2.05 us
    pallas_call x1, Pallas kernels, fast_device(): pl.pallas_call(functools.partial(unpack_kernel, capacity), out_shape=jax....  2.01 us
  transfers between devices with their start and end apart: 1, of which 1 were waited for; matrix products, arithmetic and copies ran while one was open for 0% of the time, Pallas kernels for 18%

commit v1 on v0

--- a/solution.py
+++ b/solution.py
@@ -187,19 +187,37 @@
     return route * capacity + rank
 
 
-def pack_kernel(capacity, route_ref, live_ref, query_ref, grad_ref, send_ref):
+def pack_kernel(
+    capacity, route_hbm, live_hbm, query_hbm, grad_hbm, states_hbm,
+    send_ref, held_ref, route_ref, live_ref, query_ref, grad_ref, sem,
+):
     rows, head_dim = query_ref.shape
     slots = send_ref.shape[0]
+    pairs = [
+        (route_hbm, route_ref),
+        (live_hbm, live_ref),
+        (query_hbm, query_ref),
+        (grad_hbm, grad_ref),
+        (states_hbm, held_ref),
+    ]
+    copies = [pltpu.make_async_copy(*pair, sem.at[i]) for i, pair in enumerate(pairs)]
+    for copy in copies:
+        copy.start()
+    copies[0].wait()
+    copies[1].wait()
     place = slot_row(route_ref[...], rows, capacity)
     place = jnp.where(live_ref[...] != 0, place, -1)
     pick = lax.broadcasted_iota(jnp.int32, (slots, rows), 0) == place
     pick = pick.astype(jnp.float32).astype(jnp.bfloat16)
+    copies[2].wait()
     send_ref[:, :head_dim] = jnp.dot(
         pick, query_ref[...], preferred_element_type=jnp.float32
     ).astype(jnp.bfloat16)
+    copies[3].wait()
     send_ref[:, head_dim:] = jnp.dot(
         pick, grad_ref[...], preferred_element_type=jnp.float32
     ).astype(jnp.bfloat16)
+    copies[4].wait()
 
 
 def unpack_kernel(capacity, route_ref, back_ref, out_ref):
@@ -259,9 +277,31 @@
     return value
 
 
+def load_split(xt_ref, t, head_dim):
+    half = head_dim // 2
+    return [
+        [xt_ref[t, at : at + SUB, :] for at in range(side * half, (side + 1) * half, SUB)]
+        for side in range(2)
+    ]
+
+
+def prepare(recv_ref, xt_ref, heads_held, capacity):
+    slots, width = recv_ref.shape
+    head_dim = width // 2
+    cols = slots // heads_held // LANES
+    grads = []
+    for head in range(heads_held):
+        block = head_rows(recv_ref, head, heads_held, capacity)
+        grads.append(block[:, head_dim:])
+        turned = split_query(block[:, :head_dim])
+        for col in range(cols):
+            xt_ref[head * cols + col] = turned[:, col * LANES : (col + 1) * LANES]
+    return grads
+
+
 def query_kernel(
-    heads_held, capacity, chunk, states_ref, recv_ref, out_ref,
-    state_buf, xt_ref, feat_ref, acc_ref, dqt_ref, sem,
+    heads_held, capacity, states_ref, recv_ref, out_ref,
+    xt_ref, stuffed_ref, even_ref, odd_ref, acc_ref, total_ref, dqt_ref,
 ):
     half_feat, lanes = states_ref.shape
     slots, width = recv_ref.shape
@@ -270,67 +310,82 @@
     wide = lanes // heads_held
     rows = slots // heads_held
     cols = rows // LANES
-    steps = half_feat // chunk
-    copies = [
-        pltpu.make_async_copy(
-            states_ref.at[pl.ds(i * chunk, chunk)], state_buf.at[pl.ds(i * chunk, chunk)], sem.at[i]
-        )
-        for i in range(steps)
-    ]
-    for copy in copies:
-        copy.start()
-    stuffed = []
+    piece = half_feat // cols
+    regs = half // SUB
+    runs = pair_runs(head_dim)
+    inv_root = float(np.sqrt(0.5))
+    root = float(np.sqrt(2.0))
+    feat_refs = [even_ref, odd_ref]
+    grads = prepare(recv_ref, xt_ref, heads_held, capacity)
     for head in range(heads_held):
-        block = head_rows(recv_ref, head, heads_held, capacity)
-        grad = block[:, head_dim:]
-        stuffed.append([stuff_transposed(grad, 0), stuff_transposed(grad, 1)])
-        turned = split_query(block[:, :head_dim])
-        for col in range(cols):
-            xt_ref[head * cols + col] = turned[:, col * LANES : (col + 1) * LANES]
-    for i in range(steps):
-        copies[i].wait()
-        for head in range(heads_held):
-            part = state_buf[i * chunk : (i + 1) * chunk, head * wide : (head + 1) * wide]
-            for parity in range(2):
-                feat = jnp.dot(part, stuffed[head][parity], preferred_element_type=jnp.float32)
-                for col in range(cols):
-                    feat_ref[head * cols + col, parity, i * chunk : (i + 1) * chunk, :] = feat[
-                        :, col * LANES : (col + 1) * LANES
-                    ]
-    runs = pair_runs(head_dim)
-    regs = half // SUB
-    inv_root = float(np.sqrt(0.5))
-
-    def column(t, carry):
-        values = [[xt_ref[t, p * half + m * SUB : p * half + (m + 1) * SUB, :] for m in range(regs)] for p in range(2)]
-        totals = [[jnp.zeros((SUB, LANES), jnp.float32) for _ in range(regs)] for _ in range(2)]
-        for a in range(head_dim):
+        for parity in range(2):
+            stuffed_ref[2 * head + parity] = stuff_transposed(grads[head], parity)
+
+    def expand(unit, col):
+        head, parity = divmod(unit, 2)
+        at = col * piece
+        if not isinstance(col, int):
+            at = pl.multiple_of(at, 2 * SUB)
+        feat = jnp.dot(
+            states_ref[pl.ds(at, piece), head * wide : (head + 1) * wide],
+            stuffed_ref[unit],
+            preferred_element_type=jnp.float32,
+        )
+        for other in range(cols):
+            feat_refs[parity][other, pl.ds(at, piece), :] = feat[:, other * LANES : (other + 1) * LANES]
+
+    def reduce(unit, col):
+        head, parity = divmod(unit, 2)
+        feat_ref = feat_refs[parity]
+        t = head * cols + col
+        values = load_split(xt_ref, t, head_dim)
+        if parity == 0:
+            totals = [[jnp.zeros((SUB, LANES), jnp.float32) for _ in range(regs)] for _ in range(2)]
+        else:
+            totals = load_split(total_ref, col, head_dim)
+        for a, owner, side, start, first, diagonal in runs:
+            if owner != parity:
+                continue
             at = split_place(a, head_dim)
             own = jnp.broadcast_to(xt_ref[t, at : at + 1, :], (SUB, LANES))
             acc = None
-            for owner, parity, side, start, first, diagonal in runs:
-                if owner != a:
-                    continue
-                for m in range(start // SUB, regs):
-                    place = first - start + m * SUB
-                    feat = feat_ref[t, parity, place : place + SUB, :]
-                    if m == start // SUB and (start % SUB or diagonal):
-                        feat = feat * run_weight(start % SUB, diagonal, inv_root, 1.0)
-                    term = feat * values[side][m]
-                    acc = term if acc is None else acc + term
-                    totals[side][m] = totals[side][m] + feat * own
-            acc_ref[at * SUB : (at + 1) * SUB, :] = acc
-        root = float(np.sqrt(2.0))
-        for p in range(2):
+            for m in range(start // SUB, regs):
+                place = first - start + m * SUB
+                feat = feat_ref[col, place : place + SUB, :]
+                if m == start // SUB and (start % SUB or diagonal):
+                    feat = feat * run_weight(start % SUB, diagonal, inv_root, 1.0)
+                term = feat * values[side][m]
+                acc = term if acc is None else acc + term
+                totals[side][m] = totals[side][m] + feat * own
+            acc_ref[col, parity, at * SUB : (at + 1) * SUB, :] = acc
+        owners = {a for a, owner, *_ in runs if owner == parity}
+        for a in sorted(set(range(head_dim)) - owners):
+            at = split_place(a, head_dim)
+            acc_ref[col, parity, at * SUB : (at + 1) * SUB, :] = jnp.zeros((SUB, LANES), jnp.float32)
+        for side in range(2):
             for m in range(regs):
-                total = totals[p][m]
-                base = (p * half + m * SUB) * SUB
-                for k in range(SUB):
-                    total = total + acc_ref[pl.ds(base + k, SUB, stride=SUB), :]
-                dqt_ref[t, p * half + m * SUB : p * half + (m + 1) * SUB, :] = total * root
-        return carry
-
-    lax.fori_loop(0, heads_held * cols, column, 0)
+                at = side * half + m * SUB
+                total = totals[side][m]
+                if parity == 1:
+                    for other in range(2):
+                        for k in range(SUB):
+                            total = total + acc_ref[col, other, pl.ds(at * SUB + k, SUB, stride=SUB), :]
+                    dqt_ref[t, at : at + SUB, :] = total * root
+                else:
+                    total_ref[col, at : at + SUB, :] = total
+
+    for col in range(cols):
+        expand(0, col)
+    units = 2 * heads_held
+    for unit in range(units):
+
+        def step(col, carry):
+            if unit + 1 < units:
+                expand(unit + 1, col)
+            reduce(unit, col)
+            return carry
+
+        lax.fori_loop(0, cols, step, 0)
     back = parity_split(head_dim)
     pieces = []
     for head in range(heads_held):
@@ -343,76 +398,80 @@
 
 
 def state_kernel(
-    heads_held, capacity, chunk, recv_ref, out_ref, xt_ref, feat_ref, stuffed_ref, out_buf, sem
+    heads_held, capacity, recv_ref, out_ref, xt_ref, stuffed_ref, first_ref, second_ref, out_buf, sem
 ):
     half_feat, lanes = out_ref.shape
     slots, width = recv_ref.shape
     head_dim = width // 2
-    half = head_dim // 2
     wide = lanes // heads_held
     rows = slots // heads_held
     cols = rows // LANES
-    steps = half_feat // chunk
+    piece = half_feat // cols
     runs = pair_runs(head_dim)
-    regs = half // SUB
+    regs = head_dim // 2 // SUB
     root = float(np.sqrt(2.0))
+    feat_refs = [first_ref, second_ref]
+    grads = prepare(recv_ref, xt_ref, heads_held, capacity)
     for head in range(heads_held):
-        block = head_rows(recv_ref, head, heads_held, capacity)
-        grad = block[:, head_dim:]
         for parity in range(2):
-            stuffed_ref[head, parity * rows : (parity + 1) * rows, :] = stuff(grad, parity)
-        turned = split_query(block[:, :head_dim])
-        for col in range(cols):
-            xt_ref[head * cols + col] = turned[:, col * LANES : (col + 1) * LANES]
-
-    def store_of(head, i):
+            stuffed_ref[2 * head + parity] = stuff(grads[head], parity)
+
+    def store_of(head, col):
+        at = pl.multiple_of(col * piece, SUB)
         return pltpu.make_async_copy(
-            out_buf.at[head, pl.ds(i * chunk, chunk)],
-            out_ref.at[pl.ds(i * chunk, chunk), pl.ds(head * wide, wide)],
-            sem.at[head, i],
-        )
-
-    for head in range(heads_held):
-
-        def column(col, carry):
-            t = head * cols + col
-            values = [[xt_ref[t, p * half + m * SUB : p * half + (m + 1) * SUB, :] for m in range(regs)] for p in range(2)]
-            for a, parity, side, start, first, diagonal in reversed(runs):
-                at = split_place(a, head_dim)
-                own = jnp.broadcast_to(xt_ref[t, at : at + 1, :], (SUB, LANES))
-                for m in range(start // SUB, regs):
-                    place = first - start + m * SUB
-                    value = values[side][m] * own
-                    if diagonal and m == start // SUB:
-                        value = value * run_weight(start % SUB, True, 1.0, root)
-                    else:
-                        value = value * root
-                    feat_ref[col, parity, place : place + SUB, :] = value
+            out_buf.at[head, pl.ds(at, piece)],
+            out_ref.at[pl.ds(at, piece), pl.ds(head * wide, wide)],
+            sem.at[head, col],
+        )
+
+    def expand(head, col):
+        feat_ref = feat_refs[head % 2]
+        t = head * cols + col
+        values = load_split(xt_ref, t, head_dim)
+        for a, parity, side, start, first, diagonal in reversed(runs):
+            at = split_place(a, head_dim)
+            own = jnp.broadcast_to(xt_ref[t, at : at + 1, :], (SUB, LANES))
+            for m in range(start // SUB, regs):
+                place = first - start + m * SUB
+                value = values[side][m] * own
+                if diagonal and m == start // SUB:
+                    value = value * run_weight(start % SUB, True, 1.0, root)
+                else:
+                    value = value * root
+                feat_ref[col, parity, place : place + SUB, :] = value
+
+    def product(head, col):
+        feat_ref = feat_refs[head % 2]
+        at = pl.multiple_of(col * piece, SUB)
+        total = None
+        for parity in range(2):
+            part = jnp.concatenate(
+                [feat_ref[other, parity, pl.ds(at, piece), :].astype(jnp.bfloat16) for other in range(cols)],
+                axis=1,
+            )
+            term = jnp.dot(part, stuffed_ref[2 * head + parity], preferred_element_type=jnp.float32)
+            total = term if total is None else total + term
+        out_buf[head, pl.ds(at, piece), :] = total
+
+    for head in range(heads_held + 1):
+
+        def step(col, carry):
+            if head > 0:
+                product(head - 1, col)
+            if head < heads_held:
+                expand(head, col)
+            if head > 0:
+                store_of(head - 1, col).start()
             return carry
 
-        lax.fori_loop(0, cols, column, 0)
-
-        def product(i, carry):
-            at = pl.multiple_of(i * chunk, chunk)
-            parts = [
-                feat_ref[col, parity, pl.ds(at, chunk), :].astype(jnp.bfloat16)
-                for parity in range(2)
-                for col in range(cols)
-            ]
-            out_buf[head, pl.ds(at, chunk), :] = jnp.dot(
-                jnp.concatenate(parts, axis=1), stuffed_ref[head], preferred_element_type=jnp.float32
-            )
-            store_of(head, i).start()
-            return carry
-
-        lax.fori_loop(0, steps, product, 0)
-
-    def drain(i, carry):
+        lax.fori_loop(0, cols, step, 0)
+
+    def drain(col, carry):
         for head in range(heads_held):
-            store_of(head, i).wait()
+            store_of(head, col).wait()
         return carry
 
-    lax.fori_loop(0, steps, drain, 0)
+    lax.fori_loop(0, cols, drain, 0)
 
 
 def fast_device(queries, out_grad, row_route, row_live, states):
@@ -425,49 +484,67 @@
     groups = prompt_count * KVH
     capacity = 2 * rows_here // groups
     slots = groups * capacity
-    chunk = half_feat // 6
     cols = slots // heads_held // LANES
+    units = heads_held * cols
     vmem = pl.BlockSpec(memory_space=pltpu.VMEM)
     hbm = pl.BlockSpec(memory_space=pl.ANY)
-    params = pltpu.CompilerParams(vmem_limit_bytes=60 * 1024 * 1024)
+    params = pltpu.CompilerParams(vmem_limit_bytes=48 * 1024 * 1024)
     route = row_route.reshape(1, rows_here)
     live = row_live.reshape(1, rows_here)
-    send = pl.pallas_call(
+    send, held = pl.pallas_call(
         functools.partial(pack_kernel, capacity),
-        out_shape=jax.ShapeDtypeStruct((slots, 2 * head_dim), jnp.bfloat16),
-        in_specs=[vmem] * 4,
-        out_specs=vmem,
+        out_shape=(
+            pltpu.VMEM((slots, 2 * head_dim), jnp.bfloat16),
+            pltpu.VMEM((half_feat, 2 * column_count), jnp.bfloat16),
+        ),
+        in_specs=[pl.BlockSpec(memory_space=pltpu.HBM)] * 5,
+        out_specs=(vmem, vmem),
+        scratch_shapes=[
+            pltpu.VMEM((1, rows_here), jnp.int32),
+            pltpu.VMEM((1, rows_here), jnp.int32),
+            pltpu.VMEM((rows_here, head_dim), jnp.bfloat16),
+            pltpu.VMEM((rows_here, head_dim), jnp.bfloat16),
+            pltpu.SemaphoreType.DMA((5,)),
+        ],
+        compiler_params=pltpu.CompilerParams(vmem_limit_bytes=16 * 1024 * 1024),
         name="pack_rows",
-    )(route, live, queries, out_grad)
+    )(*[
+        pltpu.with_memory_space_constraint(array, pltpu.HBM)
+        for array in (route, live, queries, out_grad, states[0])
+    ])
     recv = lax.all_to_all(send, axes, split_axis=0, concat_axis=0, tiled=True)
+    recv = pltpu.with_memory_space_constraint(recv, pltpu.VMEM)
     answer = pl.pallas_call(
-        functools.partial(query_kernel, heads_held, capacity, chunk),
+        functools.partial(query_kernel, heads_held, capacity),
         out_shape=jax.ShapeDtypeStruct((slots, head_dim), jnp.bfloat16),
-        in_specs=[hbm, vmem],
+        in_specs=[vmem, vmem],
         out_specs=vmem,
         scratch_shapes=[
-            pltpu.VMEM((half_feat, 2 * column_count), jnp.bfloat16),
-            pltpu.VMEM((heads_held * cols, head_dim, LANES), jnp.float32),
-            pltpu.VMEM((heads_held * cols, 2, half_feat, LANES), jnp.float32),
-            pltpu.VMEM((head_dim * SUB, LANES), jnp.float32),
-            pltpu.VMEM((heads_held * cols, head_dim, LANES), jnp.float32),
-            pltpu.SemaphoreType.DMA((half_feat // chunk,)),
+            pltpu.VMEM((units, head_dim, LANES), jnp.float32),
+            pltpu.VMEM((2 * heads_held, 2 * head_dim, slots // heads_held), jnp.bfloat16),
+            pltpu.VMEM((cols, half_feat, LANES), jnp.float32),
+            pltpu.VMEM((cols, half_feat, LANES), jnp.float32),
+            pltpu.VMEM((cols, 2, head_dim * SUB, LANES), jnp.float32),
+            pltpu.VMEM((cols, head_dim, LANES), jnp.float32),
+            pltpu.VMEM((units, head_dim, LANES), jnp.float32),
         ],
         compiler_params=params,
         name="query_side",
-    )(states[0], recv)
+    )(held, recv)
     back = lax.all_to_all(answer, axes, split_axis=0, concat_axis=0, tiled=True)
+    back = pltpu.with_memory_space_constraint(back, pltpu.VMEM)
     state_grad = pl.pallas_call(
-        functools.partial(state_kernel, heads_held, capacity, chunk),
+        functools.partial(state_kernel, heads_held, capacity),
         out_shape=jax.ShapeDtypeStruct((half_feat, 2 * column_count), jnp.float32),
         in_specs=[vmem],
         out_specs=hbm,
         scratch_shapes=[
-            pltpu.VMEM((heads_held * cols, head_dim, LANES), jnp.float32),
+            pltpu.VMEM((units, head_dim, LANES), jnp.float32),
+            pltpu.VMEM((2 * heads_held, slots // heads_held, 2 * head_dim), jnp.bfloat16),
             pltpu.VMEM((cols, 2, half_feat, LANES), jnp.float32),
-            pltpu.VMEM((heads_held, 2 * slots // heads_held, 2 * head_dim), jnp.bfloat16),
+            pltpu.VMEM((cols, 2, half_feat, LANES), jnp.float32),
             pltpu.VMEM((heads_held, half_feat, 2 * head_dim), jnp.float32),
-            pltpu.SemaphoreType.DMA((heads_held, half_feat // chunk)),
+            pltpu.SemaphoreType.DMA((heads_held, cols)),
         ],
         compiler_params=params,
         name="state_side",
@@ -494,7 +571,7 @@
         and column_count % head_dim == 0
         and capacity % SUB == 0
         and (groups * capacity // heads_held) % LANES == 0
-        and states.shape[1] % 96 == 0
+        and states.shape[1] % (2 * SUB * (groups * capacity // heads_held // LANES)) == 0
     )
 
 

time: 43.1 us -> 39.4 us (0.914)
  Pallas kernels: 20.9 us -> 16.2 us
  waiting for transfers between devices: 0.36 us -> 2.34 us
  local copies, waits for them, and re-layouts: 0.65 us -> 0 us
    pallas_call x3, Pallas kernels: 18.9 us -> 14.4 us  [the longest x1 6.23 us: fast_device(): pl.pallas_call(functools.partial(query_kernel, heads_held, capacity), out...]
    all_to_all x1, waiting for transfers between devices: 0.36 us -> 2.34 us  [fast_device(): back = lax.all_to_all(answer, axes, split_axis=0, concat_axis=0, tiled=True)]
    unnamed x2 -> x0, local copies, waits for them, and re-layouts: 0.65 us -> none
  transfers between devices with their start and end apart: 1 -> 1, of which waited for: 1 -> 1; matrix products, arithmetic and copies ran while one was open for 0% -> 0% of each run, Pallas kernels for 18% -> 15%
where the time goes in v1:
time: 39.4 us; the launch traced here: 39.2 us
  blocking collectives  17.4 us (44%)
  Pallas kernels  16.2 us (41%)
  starting transfers between devices  2.57 us (7%)
  waiting for transfers between devices  2.34 us (6%)
  between operations  0.66 us (2%)
    all_to_all x1, blocking collectives, fast_device(): recv = lax.all_to_all(send, axes, split_axis=0, concat_axis=0, tiled=True)  17.4 us
    pallas_call x1, Pallas kernels, fast_device(): pl.pallas_call(functools.partial(query_kernel, heads_held, capacity), out...  6.23 us
    pallas_call x1, Pallas kernels, fast_device(): pl.pallas_call(functools.partial(state_kernel, heads_held, capacity), out...  5.85 us
    all_to_all x1, starting transfers between devices, fast_device(): back = lax.all_to_all(answer, axes, split_axis=0, concat_axis=0, tiled=True)  2.57 us
    pallas_call x1, Pallas kernels, fast_device(): pl.pallas_call(functools.partial(pack_kernel, capacity), out_shape=(pltpu...  2.35 us
    all_to_all x1, waiting for transfers between devices, fast_device(): back = lax.all_to_all(answer, axes, split_axis=0, concat_axis=0, tiled=True)  2.34 us
    pallas_call x1, Pallas kernels, fast_device(): pl.pallas_call(functools.partial(unpack_kernel, capacity), out_shape=jax....  1.76 us
  transfers between devices with their start and end apart: 1, of which 1 were waited for; matrix products, arithmetic and copies ran while one was open for 0% of the time, Pallas kernels for 15%

profile of v1, /device:TPU:0, one launch (start us, length us, event | category | flops | bytes accessed | tf_op | source)
XLA Modules:
  0.0 39.2 jit_solution(17506070214641037024)
XLA Ops:
  0.6 2.4 %pack_rows.1 = (bf16[512,256]{1,0:T(8,128)(2,1)S(1)}, bf16[4128,512]{1,0:T(8,128)(2,1)S(1)}) custom-call(s32[1,256]{1,0:T(1,128)} %bitcast.14, s32[1,256]{1,0:T(1,128)} %bitcast.16, bf16[256,128]{1,0:T(8,128)(2,1)} %query_hbm.1, bf16[256,128]{1,0:T(8,128)(2,1)} %grad_hbm.1, bf16[4128,512]{1,0:T(8,128)(2,1)} %bitcast.13), custom_call_target="tpu_custom_call" | custom-call | tf_op jit(solution)/shard_map/pack_rows/pallas_call | solution.py:494
  3.0 17.4 %all_to_all.22 = bf16[32,16,256]{2,1,0:T(8,128)(2,1)S(1)} all-to-all(bf16[32,16,256]{2,1,0:T(8,128)(2,1)S(1)} %bitcast.11), channel_id=1, replica_groups=mesh['prompt'=2,'head'=16] {'prompt','head'}, dimensions={0} | all-to-all | bytes 524288 | tf_op jit(solution)/shard_map/all_to_all | solution.py:515
  20.4 6.2 %query_side.1 = bf16[512,128]{1,0:T(8,128)(2,1)} custom-call(bf16[4128,512]{1,0:T(8,128)(2,1)S(1)} %get-tuple-element.4.states_ref, bf16[512,256]{1,0:T(8,128)(2,1)S(1)} %bitcast.8), custom_call_target="tpu_custom_call" | custom-call | tf_op jit(solution)/shard_map/query_side/pallas_call | solution.py:517
  26.6 2.6 %all-to-all-start.1 = ((bf16[32,16,128]{2,1,0:T(8,128)(2,1)}), bf16[32,16,128]{2,1,0:T(8,128)(2,1)S(1)}, u32[]{:S(2)}, u32[]{:S(2)}) async-start(bf16[32,16,128]{2,1,0:T(8,128)(2,1)} %bitcast.5), calls=%async_computation.1 | async-start | bytes 262144 | tf_op jit(solution)/shard_map/all_to_all | solution.py:534
  29.2 5.9 %state_side.1 = f32[4128,512]{1,0:T(8,128)} custom-call(bf16[512,256]{1,0:T(8,128)(2,1)S(1)} %bitcast.9), custom_call_target="tpu_custom_call" | custom-call | tf_op jit(solution)/shard_map/state_side/pallas_call | solution.py:536
  35.0 2.3 %all-to-all-done.1 = bf16[32,16,128]{2,1,0:T(8,128)(2,1)S(1)} async-done(((bf16[32,16,128]{2,1,0:T(8,128)(2,1)}), bf16[32,16,128]{2,1,0:T(8,128)(2,1)S(1)}, u32[]{:S(2)}, u32[]{:S(2)}) %all-to-all-start.1) | async-done | bytes 131104 | tf_op jit(solution)/shard_map/all_to_all | solution.py:534
  37.4 1.8 %unpack_rows.1 = bf16[256,128]{1,0:T(8,128)(2,1)} custom-call(s32[1,256]{1,0:T(1,128)} %bitcast.15, bf16[512,128]{1,0:T(8,128)(2,1)S(1)} %bitcast.10), custom_call_target="tpu_custom_call" | custom-call | tf_op jit(solution)/shard_map/unpack_rows/pallas_call | solution.py:552
Async XLA Ops:
  26.6 10.8 %all-to-all-start.1 = ((bf16[32,16,128]{2,1,0:T(8,128)(2,1)}), bf16[32,16,128]{2,1,0:T(8,128)(2,1)S(1)}, u32[]{:S(2)}, u32[]{:S(2)}) async-start(bf16[32,16,128]{2,1,0:T(8,128)(2,1)} %bitcast.5), calls=%async_computation.1 | async-start | bytes 262144 | tf_op jit(solution)/shard_map/all_to_all | solution.py:534

commit v2 on v1

--- a/solution.py
+++ b/solution.py
@@ -161,7 +161,7 @@
     return (index & 1) * (head_dim // 2) + (index >> 1)
 
 
-def eye_of(size, dtype=jnp.float32):
+def eye_of(size):
     return (
         lax.broadcasted_iota(jnp.int32, (size, size), 0)
         == lax.broadcasted_iota(jnp.int32, (size, size), 1)
@@ -176,62 +176,51 @@
     return (col == wanted).astype(jnp.bfloat16)
 
 
-def slot_row(route, rows, capacity):
-    eye = eye_of(rows)
-    wide = jnp.broadcast_to(route, (rows, rows))
-    column = jnp.sum(jnp.where(eye, wide, 0), axis=1, keepdims=True)
+def slot_row(route, groups, capacity):
+    rows = route.shape[1]
+    named = lax.broadcasted_iota(jnp.int32, (groups, rows), 0) == route
+    named = named.astype(jnp.float32)
     first = lax.broadcasted_iota(jnp.int32, (rows, rows), 0)
     second = lax.broadcasted_iota(jnp.int32, (rows, rows), 1)
-    earlier = (column == wide) & (first < second)
-    rank = jnp.sum(earlier.astype(jnp.int32), axis=0, keepdims=True)
-    return route * capacity + rank
+    earlier = (first < second).astype(jnp.float32).astype(jnp.bfloat16)
+    before = jnp.dot(named.astype(jnp.bfloat16), earlier, preferred_element_type=jnp.float32)
+    rank = jnp.sum(named * before, axis=0, keepdims=True)
+    return route.astype(jnp.float32) * capacity + rank
 
 
 def pack_kernel(
     capacity, route_hbm, live_hbm, query_hbm, grad_hbm, states_hbm,
-    send_ref, held_ref, route_ref, live_ref, query_ref, grad_ref, sem,
+    send_ref, held_ref, route_ref, live_ref, pair_ref, sem,
 ):
-    rows, head_dim = query_ref.shape
+    rows, head_dim = query_hbm.shape
     slots = send_ref.shape[0]
     pairs = [
         (route_hbm, route_ref),
         (live_hbm, live_ref),
-        (query_hbm, query_ref),
-        (grad_hbm, grad_ref),
-        (states_hbm, held_ref),
+        (query_hbm, pair_ref.at[:, pl.ds(0, head_dim)]),
+        (grad_hbm, pair_ref.at[:, pl.ds(head_dim, head_dim)]),
+        (states_hbm.at[:, pl.ds(0, held_ref.shape[1])], held_ref),
     ]
     copies = [pltpu.make_async_copy(*pair, sem.at[i]) for i, pair in enumerate(pairs)]
     for copy in copies:
         copy.start()
     copies[0].wait()
     copies[1].wait()
-    place = slot_row(route_ref[...], rows, capacity)
-    place = jnp.where(live_ref[...] != 0, place, -1)
+    place = slot_row(route_ref[...], slots // capacity, capacity)
+    place = jnp.where(live_ref[...] != 0, place.astype(jnp.int32), -1)
     pick = lax.broadcasted_iota(jnp.int32, (slots, rows), 0) == place
     pick = pick.astype(jnp.float32).astype(jnp.bfloat16)
     copies[2].wait()
-    send_ref[:, :head_dim] = jnp.dot(
-        pick, query_ref[...], preferred_element_type=jnp.float32
-    ).astype(jnp.bfloat16)
     copies[3].wait()
-    send_ref[:, head_dim:] = jnp.dot(
-        pick, grad_ref[...], preferred_element_type=jnp.float32
+    send_ref[...] = jnp.dot(
+        pick, pair_ref[...], preferred_element_type=jnp.float32
     ).astype(jnp.bfloat16)
     copies[4].wait()
 
 
-def unpack_kernel(capacity, route_ref, back_ref, out_ref):
-    rows, head_dim = out_ref.shape
-    slots = back_ref.shape[0]
-    place = slot_row(route_ref[...], rows, capacity)
-    eye = eye_of(rows)
-    column = jnp.sum(
-        jnp.where(eye, jnp.broadcast_to(place, (rows, rows)), 0), axis=1, keepdims=True
-    )
-    pick = lax.broadcasted_iota(jnp.int32, (rows, slots), 1) == column
-    pick = pick.astype(jnp.float32).astype(jnp.bfloat16)
+def unpack_kernel(pick_ref, back_ref, out_ref):
     out_ref[...] = jnp.dot(
-        pick, back_ref[...], preferred_element_type=jnp.float32
+        pick_ref[...], back_ref[...], preferred_element_type=jnp.float32
     ).astype(jnp.bfloat16)
 
 
@@ -300,10 +289,10 @@
 
 
 def query_kernel(
-    heads_held, capacity, states_ref, recv_ref, out_ref,
-    xt_ref, stuffed_ref, even_ref, odd_ref, acc_ref, total_ref, dqt_ref,
+    heads_held, capacity, held_ref, recv_ref, states_hbm, out_ref,
+    rest_ref, xt_ref, stuffed_ref, even_ref, odd_ref, acc_ref, dqt_ref, sem,
 ):
-    half_feat, lanes = states_ref.shape
+    half_feat, lanes = states_hbm.shape
     slots, width = recv_ref.shape
     head_dim = width // 2
     half = head_dim // 2
@@ -316,76 +305,83 @@
     inv_root = float(np.sqrt(0.5))
     root = float(np.sqrt(2.0))
     feat_refs = [even_ref, odd_ref]
+
+    def fetch(head):
+        return pltpu.make_async_copy(
+            states_hbm.at[:, pl.ds(head * wide, wide)], rest_ref.at[head - 1], sem.at[head - 1]
+        )
+
+    for head in range(1, heads_held):
+        fetch(head).start()
     grads = prepare(recv_ref, xt_ref, heads_held, capacity)
     for head in range(heads_held):
         for parity in range(2):
             stuffed_ref[2 * head + parity] = stuff_transposed(grads[head], parity)
 
-    def expand(unit, col):
-        head, parity = divmod(unit, 2)
-        at = col * piece
-        if not isinstance(col, int):
-            at = pl.multiple_of(at, 2 * SUB)
-        feat = jnp.dot(
-            states_ref[pl.ds(at, piece), head * wide : (head + 1) * wide],
-            stuffed_ref[unit],
-            preferred_element_type=jnp.float32,
-        )
-        for other in range(cols):
-            feat_refs[parity][other, pl.ds(at, piece), :] = feat[:, other * LANES : (other + 1) * LANES]
-
-    def reduce(unit, col):
-        head, parity = divmod(unit, 2)
-        feat_ref = feat_refs[parity]
+    def expand(head, parity, start, stop):
+        rows_of = pl.ds(start, stop - start)
+        block = held_ref[rows_of] if head == 0 else rest_ref[head - 1, rows_of]
+        feat = jnp.dot(block, stuffed_ref[2 * head + parity], preferred_element_type=jnp.float32)
+        for col in range(cols):
+            feat_refs[head % 2][parity, col, rows_of] = feat[:, col * LANES : (col + 1) * LANES]
+
+    parts = 8
+    tile = 2 * SUB
+    bounds = [half_feat * i // parts // tile * tile for i in range(parts)] + [half_feat]
+    lead = 1 * half_feat // parts
+
+    def reduce(head, col, ahead):
+        feat_ref = feat_refs[head % 2]
         t = head * cols + col
         values = load_split(xt_ref, t, head_dim)
-        if parity == 0:
-            totals = [[jnp.zeros((SUB, LANES), jnp.float32) for _ in range(regs)] for _ in range(2)]
-        else:
-            totals = load_split(total_ref, col, head_dim)
-        for a, owner, side, start, first, diagonal in runs:
-            if owner != parity:
-                continue
+        totals = [[None] * regs for _ in range(2)]
+        fired = 0
+        for a in range(head_dim):
             at = split_place(a, head_dim)
             own = jnp.broadcast_to(xt_ref[t, at : at + 1, :], (SUB, LANES))
             acc = None
-            for m in range(start // SUB, regs):
-                place = first - start + m * SUB
-                feat = feat_ref[col, place : place + SUB, :]
-                if m == start // SUB and (start % SUB or diagonal):
-                    feat = feat * run_weight(start % SUB, diagonal, inv_root, 1.0)
-                term = feat * values[side][m]
-                acc = term if acc is None else acc + term
-                totals[side][m] = totals[side][m] + feat * own
-            acc_ref[col, parity, at * SUB : (at + 1) * SUB, :] = acc
-        owners = {a for a, owner, *_ in runs if owner == parity}
-        for a in sorted(set(range(head_dim)) - owners):
-            at = split_place(a, head_dim)
-            acc_ref[col, parity, at * SUB : (at + 1) * SUB, :] = jnp.zeros((SUB, LANES), jnp.float32)
+            for owner, parity, side, start, first, diagonal in runs:
+                if owner != a:
+                    continue
+                for m in range(start // SUB, regs):
+                    place = first - start + m * SUB
+                    while fired < parts and bounds[fired] < place + SUB + lead:
+                        for unit in ahead:
+                            expand(*unit, bounds[fired], bounds[fired + 1])
+                        fired += 1
+                    feat = feat_ref[parity, col, place : place + SUB, :]
+                    if m == start // SUB and (start % SUB or diagonal):
+                        feat = feat * run_weight(start % SUB, diagonal, inv_root, 1.0)
+                    term = feat * values[side][m]
+                    acc = term if acc is None else acc + term
+                    other = feat * own
+                    totals[side][m] = other if totals[side][m] is None else totals[side][m] + other
+            acc_ref[col, at * SUB : (at + 1) * SUB, :] = acc
         for side in range(2):
             for m in range(regs):
                 at = side * half + m * SUB
                 total = totals[side][m]
-                if parity == 1:
-                    for other in range(2):
-                        for k in range(SUB):
-                            total = total + acc_ref[col, other, pl.ds(at * SUB + k, SUB, stride=SUB), :]
-                    dqt_ref[t, at : at + SUB, :] = total * root
-                else:
-                    total_ref[col, at : at + SUB, :] = total
-
-    for col in range(cols):
-        expand(0, col)
-    units = 2 * heads_held
-    for unit in range(units):
-
-        def step(col, carry):
-            if unit + 1 < units:
-                expand(unit + 1, col)
-            reduce(unit, col)
-            return carry
-
-        lax.fori_loop(0, cols, step, 0)
+                for k in range(SUB):
+                    total = total + acc_ref[col, pl.ds(at * SUB + k, SUB, stride=SUB), :]
+                dqt_ref[t, at : at + SUB, :] = total * root
+
+    passes = []
+    for head in range(heads_held):
+        passes.append((head, 0, [(head, p) for p in range(2) if p == 1 or head == 0]))
+        passes.append((head, 1, [(head + 1, 0)] if head + 1 < heads_held else []))
+
+    def step(now, carry):
+        for number, (head, col, ahead) in enumerate(passes):
+
+            @pl.when(now == number)
+            def _():
+                if col == 1 and ahead:
+                    fetch(head + 1).wait()
+                reduce(head, col, ahead)
+
+        return carry
+
+    lax.fori_loop(0, len(passes), step, 0)
     back = parity_split(head_dim)
     pieces = []
     for head in range(heads_held):
@@ -398,7 +394,8 @@
 
 
 def state_kernel(
-    heads_held, capacity, recv_ref, out_ref, xt_ref, stuffed_ref, first_ref, second_ref, out_buf, sem
+    heads_held, capacity, recv_ref, route_ref, out_ref, pick_ref,
+    xt_ref, stuffed_ref, first_ref, second_ref, out_buf, sem,
 ):
     half_feat, lanes = out_ref.shape
     slots, width = recv_ref.shape
@@ -466,6 +463,14 @@
 
         lax.fori_loop(0, cols, step, 0)
 
+    here = route_ref.shape[1]
+    place = slot_row(route_ref[...], slots // capacity, capacity)
+    column = jnp.sum(
+        jnp.where(eye_of(here), jnp.broadcast_to(place, (here, here)), 0.0), axis=1, keepdims=True
+    )
+    pick = lax.broadcasted_iota(jnp.int32, (here, slots), 1) == column.astype(jnp.int32)
+    pick_ref[...] = pick.astype(jnp.float32).astype(jnp.bfloat16)
+
     def drain(col, carry):
         for head in range(heads_held):
             store_of(head, col).wait()
@@ -487,57 +492,61 @@
     cols = slots // heads_held // LANES
     units = heads_held * cols
     vmem = pl.BlockSpec(memory_space=pltpu.VMEM)
-    hbm = pl.BlockSpec(memory_space=pl.ANY)
+    hbm = pl.BlockSpec(memory_space=pltpu.HBM)
     params = pltpu.CompilerParams(vmem_limit_bytes=48 * 1024 * 1024)
     route = row_route.reshape(1, rows_here)
     live = row_live.reshape(1, rows_here)
+    inputs = [
+        pltpu.with_memory_space_constraint(array, pltpu.HBM)
+        for array in (route, live, queries, out_grad, states[0])
+    ]
     send, held = pl.pallas_call(
         functools.partial(pack_kernel, capacity),
         out_shape=(
             pltpu.VMEM((slots, 2 * head_dim), jnp.bfloat16),
-            pltpu.VMEM((half_feat, 2 * column_count), jnp.bfloat16),
+            pltpu.VMEM((half_feat, 2 * head_dim), jnp.bfloat16),
         ),
-        in_specs=[pl.BlockSpec(memory_space=pltpu.HBM)] * 5,
+        in_specs=[hbm] * 5,
         out_specs=(vmem, vmem),
         scratch_shapes=[
             pltpu.VMEM((1, rows_here), jnp.int32),
             pltpu.VMEM((1, rows_here), jnp.int32),
-            pltpu.VMEM((rows_here, head_dim), jnp.bfloat16),
-            pltpu.VMEM((rows_here, head_dim), jnp.bfloat16),
+            pltpu.VMEM((rows_here, 2 * head_dim), jnp.bfloat16),
             pltpu.SemaphoreType.DMA((5,)),
         ],
         compiler_params=pltpu.CompilerParams(vmem_limit_bytes=16 * 1024 * 1024),
         name="pack_rows",
-    )(*[
-        pltpu.with_memory_space_constraint(array, pltpu.HBM)
-        for array in (route, live, queries, out_grad, states[0])
-    ])
+    )(*inputs)
     recv = lax.all_to_all(send, axes, split_axis=0, concat_axis=0, tiled=True)
     recv = pltpu.with_memory_space_constraint(recv, pltpu.VMEM)
     answer = pl.pallas_call(
         functools.partial(query_kernel, heads_held, capacity),
         out_shape=jax.ShapeDtypeStruct((slots, head_dim), jnp.bfloat16),
-        in_specs=[vmem, vmem],
+        in_specs=[vmem, vmem, hbm],
         out_specs=vmem,
         scratch_shapes=[
+            pltpu.VMEM((max(heads_held - 1, 1), half_feat, 2 * head_dim), jnp.bfloat16),
             pltpu.VMEM((units, head_dim, LANES), jnp.float32),
             pltpu.VMEM((2 * heads_held, 2 * head_dim, slots // heads_held), jnp.bfloat16),
-            pltpu.VMEM((cols, half_feat, LANES), jnp.float32),
-            pltpu.VMEM((cols, half_feat, LANES), jnp.float32),
-            pltpu.VMEM((cols, 2, head_dim * SUB, LANES), jnp.float32),
-            pltpu.VMEM((cols, head_dim, LANES), jnp.float32),
+            pltpu.VMEM((2, cols, half_feat, LANES), jnp.float32),
+            pltpu.VMEM((2, cols, half_feat, LANES), jnp.float32),
+            pltpu.VMEM((cols, head_dim * SUB, LANES), jnp.float32),
             pltpu.VMEM((units, head_dim, LANES), jnp.float32),
+            pltpu.SemaphoreType.DMA((max(heads_held - 1, 1),)),
         ],
         compiler_params=params,
         name="query_side",
-    )(held, recv)
+    )(held, recv, inputs[4])
     back = lax.all_to_all(answer, axes, split_axis=0, concat_axis=0, tiled=True)
     back = pltpu.with_memory_space_constraint(back, pltpu.VMEM)
-    state_grad = pl.pallas_call(
+    state_grad, pick = pl.pallas_call(
         functools.partial(state_kernel, heads_held, capacity),
-        out_shape=jax.ShapeDtypeStruct((half_feat, 2 * column_count), jnp.float32),
-        in_specs=[vmem],
-        out_specs=hbm,
+        out_shape=(
+            jax.ShapeDtypeStruct((half_feat, 2 * column_count), jnp.float32),
+            pltpu.VMEM((rows_here, slots), jnp.bfloat16),
+        ),
+        in_specs=[vmem, vmem],
+        out_specs=(hbm, vmem),
         scratch_shapes=[
             pltpu.VMEM((units, head_dim, LANES), jnp.float32),
             pltpu.VMEM((2 * heads_held, slots // heads_held, 2 * head_dim), jnp.bfloat16),
@@ -548,14 +557,15 @@
         ],
         compiler_params=params,
         name="state_side",
-    )(recv)
+    )(recv, route)
+    pick = pltpu.with_memory_space_constraint(pick, pltpu.VMEM)
     query_grad = pl.pallas_call(
-        functools.partial(unpack_kernel, capacity),
+        unpack_kernel,
         out_shape=jax.ShapeDtypeStruct((rows_here, head_dim), jnp.bfloat16),
         in_specs=[vmem] * 2,
         out_specs=vmem,
         name="unpack_rows",
-    )(route, back)
+    )(pick, back)
     return (query_grad, state_grad[None])
 
 
@@ -570,7 +580,7 @@
         and heads_held >= 1
         and column_count % head_dim == 0
         and capacity % SUB == 0
-        and (groups * capacity // heads_held) % LANES == 0
+        and groups * capacity // heads_held == 2 * LANES
         and states.shape[1] % (2 * SUB * (groups * capacity // heads_held // LANES)) == 0
     )
 

time: 39.4 us -> 37.4 us (0.949)
  Pallas kernels: 16.2 us -> 14.2 us
    pallas_call x1, Pallas kernels: 1.76 us -> 0.85 us  [fast_device(): pl.pallas_call(unpack_kernel, out_shape=jax.ShapeDtypeStruct((rows_here,...]
    pallas_call x1, Pallas kernels: 2.35 us -> 1.75 us  [fast_device(): pl.pallas_call(functools.partial(pack_kernel, capacity), out_shape=(pltpu...]
    pallas_call x1, Pallas kernels: 6.23 us -> 5.74 us  [fast_device(): pl.pallas_call(functools.partial(query_kernel, heads_held, capacity), out...]
  transfers between devices with their start and end apart: 1 -> 1, of which waited for: 1 -> 1; matrix products, arithmetic and copies ran while one was open for 0% -> 0% of each run, Pallas kernels for 15% -> 16%
where the time goes in v2:
time: 37.4 us; the launch traced here: 37.2 us
  blocking collectives  17.4 us (47%)
  Pallas kernels  14.2 us (38%)
  starting transfers between devices  2.58 us (7%)
  waiting for transfers between devices  2.33 us (6%)
  between operations  0.68 us (2%)
    all_to_all x1, blocking collectives, fast_device(): recv = lax.all_to_all(send, axes, split_axis=0, concat_axis=0, tiled=True)  17.4 us
    pallas_call x1, Pallas kernels, fast_device(): pl.pallas_call(functools.partial(state_kernel, heads_held, capacity), out...  5.86 us
    pallas_call x1, Pallas kernels, fast_device(): pl.pallas_call(functools.partial(query_kernel, heads_held, capacity), out...  5.74 us
    all_to_all x1, starting transfers between devices, fast_device(): back = lax.all_to_all(answer, axes, split_axis=0, concat_axis=0, tiled=True)  2.58 us
    all_to_all x1, waiting for transfers between devices, fast_device(): back = lax.all_to_all(answer, axes, split_axis=0, concat_axis=0, tiled=True)  2.33 us
    pallas_call x1, Pallas kernels, fast_device(): pl.pallas_call(functools.partial(pack_kernel, capacity), out_shape=(pltpu...  1.75 us
    pallas_call x1, Pallas kernels, fast_device(): pl.pallas_call(unpack_kernel, out_shape=jax.ShapeDtypeStruct((rows_here,...  0.85 us
  transfers between devices with their start and end apart: 1, of which 1 were waited for; matrix products, arithmetic and copies ran while one was open for 0% of the time, Pallas kernels for 16%

profile of v2, /device:TPU:0, one launch (start us, length us, event | category | flops | bytes accessed | tf_op | source)
XLA Modules:
  0.0 37.2 jit_solution(8818094873680209984)
XLA Ops:
  0.6 1.8 %pack_rows.1 = (bf16[512,256]{1,0:T(8,128)(2,1)S(1)}, bf16[4128,256]{1,0:T(8,128)(2,1)S(1)}) custom-call(s32[1,256]{1,0:T(1,128)} %bitcast.12, s32[1,256]{1,0:T(1,128)} %bitcast.16, bf16[256,128]{1,0:T(8,128)(2,1)} %query_hbm.1, bf16[256,128]{1,0:T(8,128)(2,1)} %grad_hbm.1, bf16[4128,512]{1,0:T(8,128)(2,1)} %bitcast.14), custom_call_target="tpu_custom_call" | custom-call | tf_op jit(solution)/shard_map/pack_rows/pallas_call | solution.py:503
  2.4 0.0 copy-start
  2.4 17.4 %all_to_all.22 = bf16[32,16,256]{2,1,0:T(8,128)(2,1)S(1)} all-to-all(bf16[32,16,256]{2,1,0:T(8,128)(2,1)S(1)} %bitcast.11), channel_id=1, replica_groups=mesh['prompt'=2,'head'=16] {'prompt','head'}, dimensions={0} | all-to-all | bytes 524288 | tf_op jit(solution)/shard_map/all_to_all | solution.py:520
  19.8 5.7 %query_side.1 = bf16[512,128]{1,0:T(8,128)(2,1)} custom-call(bf16[4128,256]{1,0:T(8,128)(2,1)S(1)} %get-tuple-element.8.held_ref, bf16[512,256]{1,0:T(8,128)(2,1)S(1)} %bitcast.8, bf16[4128,512]{1,0:T(8,128)(2,1)} %bitcast.15), custom_call_target="tpu_custom_call" | custom-call | tf_op jit(solution)/shard_map/query_side/pallas_call | solution.py:522
  25.5 2.6 %all-to-all-start.1 = ((bf16[32,16,128]{2,1,0:T(8,128)(2,1)}), bf16[32,16,128]{2,1,0:T(8,128)(2,1)S(1)}, u32[]{:S(2)}, u32[]{:S(2)}) async-start(bf16[32,16,128]{2,1,0:T(8,128)(2,1)} %bitcast.5), calls=%async_computation.1 | async-start | bytes 262144 | tf_op jit(solution)/shard_map/all_to_all | solution.py:540
  28.1 0.0 copy-done
  28.1 5.9 %state_side.1 = (f32[4128,512]{1,0:T(8,128)}, bf16[256,512]{1,0:T(8,128)(2,1)S(1)}) custom-call(bf16[512,256]{1,0:T(8,128)(2,1)S(1)} %bitcast.9, s32[1,256]{1,0:T(1,128)S(1)} %bitcast.13), custom_call_target="tpu_custom_call" | custom-call | tf_op jit(solution)/shard_map/state_side/pallas_call | solution.py:542
  34.0 2.3 %all-to-all-done.1 = bf16[32,16,128]{2,1,0:T(8,128)(2,1)S(1)} async-done(((bf16[32,16,128]{2,1,0:T(8,128)(2,1)}), bf16[32,16,128]{2,1,0:T(8,128)(2,1)S(1)}, u32[]{:S(2)}, u32[]{:S(2)}) %all-to-all-start.1) | async-done | bytes 131104 | tf_op jit(solution)/shard_map/all_to_all | solution.py:540
  36.3 0.8 %unpack_rows.1 = bf16[256,128]{1,0:T(8,128)(2,1)} custom-call(bf16[256,512]{1,0:T(8,128)(2,1)S(1)} %get-tuple-element.7.pick_ref, bf16[512,128]{1,0:T(8,128)(2,1)S(1)} %bitcast.10), custom_call_target="tpu_custom_call" | custom-call | tf_op jit(solution)/shard_map/unpack_rows/pallas_call | solution.py:562
Async XLA Ops:
  2.4 25.7 %copy-start = (s32[256,1]{0,1:T(1,128)S(1)}, s32[256,1]{0,1:T(1,128)}, u32[]{:S(2)}) copy-start(s32[256,1]{0,1:T(1,128)} %param.7) | copy-start | bytes 3076
  25.5 10.8 %all-to-all-start.1 = ((bf16[32,16,128]{2,1,0:T(8,128)(2,1)}), bf16[32,16,128]{2,1,0:T(8,128)(2,1)S(1)}, u32[]{:S(2)}, u32[]{:S(2)}) async-start(bf16[32,16,128]{2,1,0:T(8,128)(2,1)} %bitcast.5), calls=%async_computation.1 | async-start | bytes 262144 | tf_op jit(solution)/shard_map/all_to_all | solution.py:540
